TPU v7x, 256 devices: a whole 4x4x8 slice. The times are simulated.
256 devices in a mesh: region: 8 (over x, core), dom: 32 (over z, y).
Axes of the slice: x: 4, y: 4, z: 8, core: 2. Of those that a mesh axis runs over, the one named last changes fastest.
Arguments:
- x_init: bfloat16 [1048576, 128], P(('region', 'dom')), may hold values from -6 to 6
- tiles: bfloat16 [73728, 128, 128], P(('region', 'dom'))
- tile_row: int32 [73728], P(('region', 'dom')), may hold values from 0 to 31
- tile_col: int32 [73728], P(('region', 'dom')), may hold values from 0 to 63, as said below
- send_list: int32 [256, 4, 8], P(('region', 'dom')), may hold values from 0 to 31, as said below
- send_count: int32 [256, 4], P(('region', 'dom')), may hold values from 1 to 8, as said below
Outputs:
- basis: bfloat16 [1048576, 128], P(('region', 'dom'))
- ritz_matrix: float32 [2, 128, 128], replicated
Inputs may be any that keep to these rules, and one draw needn't show every extreme that they name: `send_list`: the 8 entries of one partition and direction are distinct row tiles of that partition. `send_count`: some partition sends 8 row tiles in every direction. `tile_col`: a value 32 + d * 8 + s with d = 0 .. 3 names slot s of the d-th received stack of extended, and s is below the count that this neighbour sends; no value names a stack where the neighbour does not exist.
All inputs are finite; a program needn't handle non-finite values.
Results may differ from a plain program's by a relative error of at most 0.00115.
The roundings to bfloat16 on the way count: a program that leaves them out, or rounds other values in their place, can miss the bound.
Values may be sent and summed in bfloat16 or wider, within the bound.
No kernel may reach another device: no remote copies, remote signals or barrier semaphores. Data moves between devices by JAX's collectives and lax.ppermute only.
A program may use at most 64 MiB of HBM per device.

v0:
```python
import math
import jax
import jax.numpy as jnp
from jax import lax
from jax.sharding import PartitionSpec as P

ITERS = 2
HIGH = lax.Precision.HIGHEST


def shifted(block, axis, distance):
    devices = range(lax.axis_size(axis))
    route = [(i - distance, i) for i in devices if i - distance in devices]
    return lax.ppermute(block, axis, route)


def local_gram(current, node_total):
    return (
        lax.dot_general(
            current, current, (((0,), (0,)), ((), ())), preferred_element_type=jnp.float32
        )
        / node_total
    )


def rayleigh_sum(partial_value):
    return lax.psum(partial_value, ("region", "dom"))


def pass_dom(packed, offset):
    return shifted(packed, "dom", offset)


def pass_region(packed, offset):
    return shifted(packed, "region", offset)


def apply_graph(basis, tiles, tile_row, tile_col, send_rows, live_slot, row_tiles, tile_size):
    vectors = basis.shape[1]
    blocks = basis.reshape(row_tiles, tile_size, vectors)
    picked = blocks[send_rows]
    packed = jnp.where(live_slot[:, :, None, None], picked, jnp.zeros_like(picked))
    received = [
        pass_dom(packed[0], 1),
        pass_dom(packed[1], -1),
        pass_region(packed[2], 1),
        pass_region(packed[3], -1),
    ]
    extended = jnp.concatenate([blocks] + received, axis=0)
    group = 32
    group_count = tiles.shape[0] // group
    tile_groups = tiles.reshape(group_count, group, tile_size, tile_size)
    col_groups = tile_col.reshape(group_count, group)
    row_groups = tile_row.reshape(group_count, group)
    row_ids = jnp.arange(row_tiles, dtype=jnp.int32)

    def add_group(accumulated, pieces):
        tile_part, col_part, row_part = pieces
        gathered = extended[col_part]
        products = lax.dot_general(
            tile_part, gathered, (((2,), (1,)), ((0,), (0,))), preferred_element_type=jnp.float32
        )
        select = (row_part[None, :] == row_ids[:, None]).astype(jnp.float32)
        return (accumulated + jnp.einsum("rt,tiw->riw", select, products, precision=HIGH), None)

    start = jnp.zeros((row_tiles, tile_size, vectors), jnp.float32)
    applied, _ = lax.scan(add_group, start, (tile_groups, col_groups, row_groups))
    return applied.reshape(row_tiles * tile_size, vectors)


def shards(x_init, tiles, tile_row, tile_col, send_list, send_count):
    row_count, vectors = x_init.shape
    tile_size = tiles.shape[1]
    row_tiles = row_count // tile_size
    capacity = send_list.shape[2]
    node_total = row_count * lax.axis_size("region") * lax.axis_size("dom")
    root_total = math.sqrt(node_total)
    send_rows = send_list[0]
    live_slot = jnp.arange(capacity, dtype=jnp.int32)[None, :] < send_count[0][:, None]
    identity = jnp.eye(vectors, dtype=jnp.float32)
    current = x_init
    gram = lax.psum(local_gram(current, node_total), ("region", "dom"))
    rayleigh_list = []
    basis = x_init
    for iteration in range(ITERS):
        factor = jnp.linalg.cholesky(gram)
        inverse = lax.linalg.triangular_solve(factor, identity, left_side=True, lower=True)
        basis = jnp.dot(current.astype(jnp.float32), inverse.T, precision=HIGH).astype(jnp.bfloat16)
        applied = apply_graph(
            basis, tiles, tile_row, tile_col, send_rows, live_slot, row_tiles, tile_size
        )
        partial_value = jnp.dot(basis.astype(jnp.float32).T, applied, precision=HIGH) / root_total
        if iteration + 1 < ITERS:
            current = applied.astype(jnp.bfloat16)
            rayleigh_list.append(rayleigh_sum(partial_value))
            gram = lax.psum(local_gram(current, node_total), ("region", "dom"))
        else:
            rayleigh_list.append(rayleigh_sum(partial_value))
    return (basis, jnp.stack(rayleigh_list))


def solution(mesh):
    in_specs = (
        P(("region", "dom"), None),
        P(("region", "dom"), None, None),
        P(("region", "dom")),
        P(("region", "dom")),
        P(("region", "dom"), None, None),
        P(("region", "dom"), None),
    )
    out_specs = (P(("region", "dom"), None), P())
    return jax.shard_map(shards, mesh=mesh, in_specs=in_specs, out_specs=out_specs, check_vma=False)
```

profile of v0, /device:TPU:2, one launch (start us, length us, event | category | flops | bytes accessed | tf_op | source)
XLA Modules:
  0.0 1021.1 jit_solution(12112515196211047036)
XLA Ops:
  9.8 247.8 %all-reduce.5.cloned.1.call-done = f32[128,128]{0,1:T(8,128)} async-done(((f32[128,128]{0,1:T(8,128)}), f32[128,128]{0,1:T(8,128)}) %all-reduce.5.cloned.1.call-update) | async-done | bytes 65552 | tf_op jit(solution)/shard_map/psum | solution.py:82
  259.4 11.7 %cholesky.44 = f32[128,128]{1,0:T(8,128)S(1)} custom-call(f32[128,128]{1,0:T(8,128)S(1)} %fusion.46), custom_call_target="Cholesky" | custom-call | tf_op jit(solution)/shard_map/jit(cholesky)/cholesky | solution.py:86
  272.4 9.8 custom-call.8
  295.1 3.3 collective-permute-start.3
  298.5 3.4 collective-permute-done.1
  303.6 82.5 %while.22 = (s32[]{:T(128)}, f32[32,128,128]{2,0,1:T(8,128)}, s32[9,32]{1,0:T(8,128)S(1)}, bf16[9,32,128,128]{3,2,1,0:T(8,128)(2,1)}, s32[9,32]{1,0:T(8,128)S(1)...) while((s32[]{:T(128)}, f32[32,128,128]{2,0,1:T(8,128)}, s32[9,32]{1,0:T(8,128)S(1)}, ...), condition=%wide.region_4.7_spmd.clone, body=%wide.region_3.6_spmd.clone.sunk | while | flops 336595040 | bytes 29365292 | solution.py:67
  307.8 3.5 select_add_fusion.4
  317.0 3.5 select_add_fusion.4
  326.2 3.5 select_add_fusion.4
  335.4 3.5 select_add_fusion.4
  344.5 3.5 select_add_fusion.4
  353.7 3.5 select_add_fusion.4
  362.9 3.5 select_add_fusion.4
  372.0 3.5 select_add_fusion.4
  381.2 3.5 select_add_fusion.4
  386.1 3.5 fusion.32
  392.2 239.2 %all-reduce.7.cloned.1.call-done = f32[128,128]{0,1:T(8,128)} async-done(((f32[128,128]{0,1:T(8,128)}), f32[128,128]{0,1:T(8,128)}) %all-reduce.7.cloned.1.call-update) | async-done | bytes 65552 | tf_op jit(solution)/shard_map/psum | solution.py:96
  633.2 11.7 %cholesky.55 = f32[128,128]{1,0:T(8,128)S(1)} custom-call(f32[128,128]{1,0:T(8,128)S(1)} %fusion.44), custom_call_target="Cholesky" | custom-call | tf_op jit(solution)/shard_map/jit(cholesky)/cholesky | solution.py:86
  646.3 9.8 custom-call.9
  661.5 4.6 collective-permute-start.4
  670.0 3.9 collective-permute-start.7
  678.8 82.3 %while.23 = (s32[]{:T(128)}, f32[32,128,128]{2,0,1:T(8,128)}, s32[9,32]{1,0:T(8,128)S(1)}, bf16[9,32,128,128]{3,2,1,0:T(8,128)(2,1)}, s32[9,32]{1,0:T(8,128)S(1)...) while((s32[]{:T(128)}, f32[32,128,128]{2,0,1:T(8,128)}, s32[9,32]{1,0:T(8,128)S(1)}, ...), condition=%wide.region_8.11_spmd.clone, body=%wide.region_7.10_spmd.clone.sunk | while | flops 336595040 | bytes 29365292 | solution.py:67
  683.1 3.5 select_add_fusion.5
  692.2 3.5 select_add_fusion.5
  701.4 3.5 select_add_fusion.5
  710.5 3.5 select_add_fusion.5
  719.7 3.5 select_add_fusion.5
  728.8 3.5 select_add_fusion.5
  738.0 3.5 select_add_fusion.5
  747.1 3.5 select_add_fusion.5
  756.3 3.5 select_add_fusion.5
  766.0 247.0 %all-reduce.9.cloned.1.call-done = (f32[1,128,128]{2,1,0:T(8,128)}, f32[1,128,128]{2,1,0:T(8,128)}) async-done(((f32[1,128,128]{2,1,0:T(8,128)}, f32[1,128,128]{2,1,0:T(8,128)}), (f32[1,128,128]{2,1,0:T(8,128)}, f32[1,128,128]{2,1,0:T(8,128)})) %all-reduce.9.cloned.1.call-update) | async-done | bytes 131088 | tf_op jit(solution)/shard_map/psum | solution.py:27
  (249 shorter events, 147.0 us)
Async XLA Ops:
  7.2 2.4 copy-start.15
  7.2 2.5 copy-start.14
  7.2 250.4 %all-reduce.5.cloned.1.call-start = ((), (), s32[]{:S(2)}) async-start(), calls=%async_computation | async-start | bytes 131072 | tf_op jit(solution)/shard_map/psum | solution.py:82
  9.5 621.9 %all-reduce.7.cloned.1.call-start = ((), (), s32[]{:S(2)}) async-start(), calls=%async_computation.1 | async-start | bytes 131072 | tf_op jit(solution)/shard_map/psum | solution.py:96
  283.5 2.3 copy-start.10
  285.9 6.6 copy-start.12
  285.9 6.7 copy-start.13
  288.2 10.3 %collective-permute-start = (bf16[8,128,128]{2,1,0:T(8,128)(2,1)}, bf16[8,128,128]{2,1,0:T(8,128)(2,1)S(1)}, u32[]{:S(2)}, u32[]{:S(2)}) collective-permute-start(bf16[8,128,128]{2,1,0:T(8,128)(2,1)} %get-tuple-element.159), channel_id=1, source_target_pairs={{0,1},{1,2},{2,3},{3,4},{4,5},{5,6},{6,7},{7,8},{8,9},{9,10},{10,1... | collective-permute-start | bytes 786440 | tf_op jit(solution)/shard_map/ppermute | solution.py:14
  291.2 10.8 %collective-permute-start.1 = (bf16[8,128,128]{2,1,0:T(8,128)(2,1)}, bf16[8,128,128]{2,1,0:T(8,128)(2,1)S(1)}, u32[]{:S(2)}, u32[]{:S(2)}) collective-permute-start(bf16[8,128,128]{2,1,0:T(8,128)(2,1)} %get-tuple-element.158), channel_id=1, source_target_pairs={{1,0},{2,1},{3,2},{4,3},{5,4},{6,5},{7,6},{8,7},{9,8},{10,9},{11,1... | collective-permute-start | bytes 786440 | tf_op jit(solution)/shard_map/ppermute | solution.py:14
  292.6 9.4 collective-permute-start.2
  295.1 7.0 collective-permute-start.3
  305.9 1.9 copy-start.1
  315.1 1.9 copy-start.1
  324.3 1.9 copy-start.1
  333.4 1.9 copy-start.1
  342.6 1.9 copy-start.1
  351.8 1.9 copy-start.1
  360.9 1.9 copy-start.1
  386.1 3.6 copy-start.3
  389.6 623.4 %all-reduce.9.cloned.1.call-start = ((), (), s32[]{:S(2)}) async-start(), calls=%async_computation.2 | async-start | bytes 262144 | tf_op jit(solution)/shard_map/psum | solution.py:27
  659.0 105.0 %copy-start.9 = (bf16[4096,128]{1,0:T(8,128)(2,1)}, bf16[4096,128]{1,0:T(8,128)(2,1)S(1)}, u32[]{:S(2)}) copy-start(bf16[4096,128]{1,0:T(8,128)(2,1)S(1)} %convolution_convert_fusion) | copy-start | bytes 3145732
  659.7 6.3 copy-start.8
  659.8 6.3 copy-start.11
  660.0 13.9 %collective-permute-start.5 = (bf16[8,128,128]{2,1,0:T(8,128)(2,1)S(1)}, bf16[8,128,128]{2,1,0:T(8,128)(2,1)S(1)}, u32[]{:S(2)}, u32[]{:S(2)}) collective-permute-start(bf16[8,128,128]{2,1,0:T(8,128)(2,1)S(1)} %get-tuple-element.154), channel_id=1, source_target_pairs={{1,0},{2,1},{3,2},{4,3},{5,4},{6,5},{7,6},{8,7},{9,8},{10,9},{11,1... | collective-permute-start | bytes 786440 | tf_op jit(solution)/shard_map/ppermute | solution.py:14
  661.5 12.4 %collective-permute-start.4 = (bf16[8,128,128]{2,1,0:T(8,128)(2,1)S(1)}, bf16[8,128,128]{2,1,0:T(8,128)(2,1)S(1)}, u32[]{:S(2)}, u32[]{:S(2)}) collective-permute-start(bf16[8,128,128]{2,1,0:T(8,128)(2,1)S(1)} %get-tuple-element.155), channel_id=1, source_target_pairs={{0,1},{1,2},{2,3},{3,4},{4,5},{5,6},{6,7},{7,8},{8,9},{9,10},{10,1... | collective-permute-start | bytes 786440 | tf_op jit(solution)/shard_map/ppermute | solution.py:14
  667.9 7.7 collective-permute-start.6
  670.0 7.5 collective-permute-start.7
  681.2 1.9 copy-start.4
  690.3 1.9 copy-start.4
  726.9 1.9 copy-start.4
  736.1 1.9 copy-start.4
  745.2 1.9 copy-start.4
  (27 other events, 39.6 us)
Sparse Core Ops, SparseCore 0:
  14.1 243.4 all-reduce.4
  389.7 241.6 all-reduce.6
  766.1 246.8 all-reduce.8
where the time goes:
time: 1020 us
  waiting for transfers between devices  741 us (73%)
  matrix products  108 us (11%)
  local copies, waits for them, and re-layouts  83.8 us (8%)
  other arithmetic  50.8 us (5%)
  starting transfers between devices  21.9 us (2%)
  between operations  14.2 us (1%)
    psum x2, waiting for transfers between devices, shards(): gram = lax.psum(local_gram(current, node_total), ('region', 'dom'))  487 us
    psum x1, waiting for transfers between devices, rayleigh_sum(): return lax.psum(partial_value, ('region', 'dom'))  247 us
    dot_general x18, matrix products, add_group(): jnp.einsum('rt,tiw->riw', select, products, precision=HIGH)  63.3 us
    gather x18, local copies, waits for them, and re-layouts, add_group(): gathered = extended[col_part]  42.1 us
    dot_general x18, matrix products, add_group(): lax.dot_general(tile_part, gathered, (((2,), (1,)), ((0,), (0,))), prefer...  32.4 us
    while x72, local copies, waits for them, and re-layouts  25.8 us
    another operation x6, other arithmetic, shards(): factor = jnp.linalg.cholesky(gram)  24.8 us
    ppermute x8, starting transfers between devices, shifted(): return lax.ppermute(block, axis, route)  21.8 us
  transfers between devices with their start and end apart: 11, of which 7 were waited for; matrix products, arithmetic and copies ran while one was open for 1% of the time, Pallas kernels for 0%

commit v1 on v0

--- a/solution.py
+++ b/solution.py
@@ -24,7 +24,7 @@
 
 
 def rayleigh_sum(partial_value):
-    return lax.psum(partial_value, ("region", "dom"))
+    return lax.psum(lax.psum(partial_value, "dom"), "region")
 
 
 def pass_dom(packed, offset):

time: 1020 us -> 985 us (0.966)
  waiting for transfers between devices: 741 us -> 701 us
    psum x1 -> x2, waiting for transfers between devices: 247 us -> 207 us  [rayleigh_sum(): return lax.psum(lax.psum(partial_value, 'dom'), 'region')]
  transfers between devices with their start and end apart: 11 -> 12, of which waited for: 7 -> 8; matrix products, arithmetic and copies ran while one was open for 1% -> 1% of each run, Pallas kernels for 0% -> 0%
where the time goes in v1:
time: 985 us; the launch traced here: 981 us
  waiting for transfers between devices  701 us (71%)
  matrix products  108 us (11%)
  local copies, waits for them, and re-layouts  83.8 us (9%)
  other arithmetic  50.8 us (5%)
  starting transfers between devices  21.9 us (2%)
  between operations  14.2 us (1%)
    psum x2, waiting for transfers between devices, shards(): gram = lax.psum(local_gram(current, node_total), ('region', 'dom'))  487 us
    psum x2, waiting for transfers between devices, rayleigh_sum(): return lax.psum(lax.psum(partial_value, 'dom'), 'region')  207 us
    dot_general x18, matrix products, add_group(): jnp.einsum('rt,tiw->riw', select, products, precision=HIGH)  63.3 us
    gather x18, local copies, waits for them, and re-layouts, add_group(): gathered = extended[col_part]  42.1 us
    dot_general x18, matrix products, add_group(): lax.dot_general(tile_part, gathered, (((2,), (1,)), ((0,), (0,))), prefer...  32.4 us
    while x72, local copies, waits for them, and re-layouts  25.8 us
    another operation x6, other arithmetic, shards(): factor = jnp.linalg.cholesky(gram)  24.8 us
    ppermute x8, starting transfers between devices, shifted(): return lax.ppermute(block, axis, route)  21.8 us
  transfers between devices with their start and end apart: 12, of which 8 were waited for; matrix products, arithmetic and copies ran while one was open for 1% of the time, Pallas kernels for 0%

profile of v1, /device:TPU:2, one launch (start us, length us, event | category | flops | bytes accessed | tf_op | source)
XLA Modules:
  0.0 981.4 jit_solution(18150699073633119909)
XLA Ops:
  9.8 247.8 %all-reduce.7.cloned.1.call-done = f32[128,128]{0,1:T(8,128)} async-done(((f32[128,128]{0,1:T(8,128)}), f32[128,128]{0,1:T(8,128)}) %all-reduce.7.cloned.1.call-update) | async-done | bytes 65552 | tf_op jit(solution)/shard_map/psum | solution.py:82
  259.4 11.7 %cholesky.44 = f32[128,128]{1,0:T(8,128)S(1)} custom-call(f32[128,128]{1,0:T(8,128)S(1)} %fusion.44), custom_call_target="Cholesky" | custom-call | tf_op jit(solution)/shard_map/jit(cholesky)/cholesky | solution.py:86
  272.4 9.8 custom-call.8
  298.5 3.4 collective-permute-done.1
  303.5 82.5 %while.22 = (s32[]{:T(128)}, f32[32,128,128]{2,0,1:T(8,128)}, s32[9,32]{1,0:T(8,128)S(1)}, bf16[9,32,128,128]{3,2,1,0:T(8,128)(2,1)}, s32[9,32]{1,0:T(8,128)S(1)...) while((s32[]{:T(128)}, f32[32,128,128]{2,0,1:T(8,128)}, s32[9,32]{1,0:T(8,128)S(1)}, ...), condition=%wide.region_4.7_spmd.clone, body=%wide.region_3.6_spmd.clone.sunk | while | flops 336595040 | bytes 29365292 | solution.py:67
  307.8 3.5 select_add_fusion.4
  317.0 3.5 select_add_fusion.4
  326.2 3.5 select_add_fusion.4
  335.3 3.5 select_add_fusion.4
  344.5 3.5 select_add_fusion.4
  353.7 3.5 select_add_fusion.4
  362.8 3.5 select_add_fusion.4
  372.0 3.5 select_add_fusion.4
  381.2 3.5 select_add_fusion.4
  386.1 3.5 fusion.32
  392.2 239.2 %all-reduce.9.cloned.1.call-done = f32[128,128]{0,1:T(8,128)} async-done(((f32[128,128]{0,1:T(8,128)}), f32[128,128]{0,1:T(8,128)}) %all-reduce.9.cloned.1.call-update) | async-done | bytes 65552 | tf_op jit(solution)/shard_map/psum | solution.py:96
  633.2 11.7 %cholesky.55 = f32[128,128]{1,0:T(8,128)S(1)} custom-call(f32[128,128]{1,0:T(8,128)S(1)} %fusion.42), custom_call_target="Cholesky" | custom-call | tf_op jit(solution)/shard_map/jit(cholesky)/cholesky | solution.py:86
  646.3 9.8 custom-call.9
  661.5 4.6 collective-permute-start.4
  670.0 3.9 collective-permute-start.7
  678.8 82.3 %while.23 = (s32[]{:T(128)}, f32[32,128,128]{2,0,1:T(8,128)}, s32[9,32]{1,0:T(8,128)S(1)}, bf16[9,32,128,128]{3,2,1,0:T(8,128)(2,1)}, s32[9,32]{1,0:T(8,128)S(1)...) while((s32[]{:T(128)}, f32[32,128,128]{2,0,1:T(8,128)}, s32[9,32]{1,0:T(8,128)S(1)}, ...), condition=%wide.region_9.12_spmd.clone, body=%wide.region_8.11_spmd.clone.sunk | while | flops 336595040 | bytes 29365292 | solution.py:67
  683.1 3.5 select_add_fusion.5
  692.3 3.5 select_add_fusion.5
  701.4 3.5 select_add_fusion.5
  710.6 3.5 select_add_fusion.5
  719.7 3.5 select_add_fusion.5
  728.8 3.5 select_add_fusion.5
  738.0 3.5 select_add_fusion.5
  747.1 3.5 select_add_fusion.5
  756.3 3.5 select_add_fusion.5
  766.1 143.6 %all-reduce.11.cloned.1.call-done = (f32[128,128]{1,0:T(8,128)}, f32[128,128]{1,0:T(8,128)}) async-done(((f32[128,128]{1,0:T(8,128)}, f32[128,128]{1,0:T(8,128)}), (f32[128,128]{1,0:T(8,128)}, f32[128,128]{1,0:T(8,128)})) %all-reduce.11.cloned.1.call-update) | async-done | bytes 131088 | tf_op jit(solution)/shard_map/psum | solution.py:27
  909.7 63.6 %all-reduce.13.cloned.1.call-done = (f32[1,128,128]{2,1,0:T(8,128)}, f32[1,128,128]{2,1,0:T(8,128)}) async-done(((f32[1,128,128]{2,1,0:T(8,128)}, f32[1,128,128]{2,1,0:T(8,128)}), (f32[1,128,128]{2,1,0:T(8,128)}, f32[1,128,128]{2,1,0:T(8,128)})) %all-reduce.13.cloned.1.call-update) | async-done | bytes 131088 | tf_op jit(solution)/shard_map/psum | solution.py:27
  (252 shorter events, 150.4 us)
Async XLA Ops:
  7.2 2.4 copy-start.15
  7.2 2.5 copy-start.14
  7.2 250.4 %all-reduce.7.cloned.1.call-start = ((), (), s32[]{:S(2)}) async-start(), calls=%async_computation | async-start | bytes 131072 | tf_op jit(solution)/shard_map/psum | solution.py:82
  9.5 621.9 %all-reduce.9.cloned.1.call-start = ((), (), s32[]{:S(2)}) async-start(), calls=%async_computation.1 | async-start | bytes 131072 | tf_op jit(solution)/shard_map/psum | solution.py:96
  283.5 2.3 copy-start.10
  285.9 6.6 copy-start.12
  285.9 6.7 copy-start.13
  288.2 10.3 %collective-permute-start = (bf16[8,128,128]{2,1,0:T(8,128)(2,1)}, bf16[8,128,128]{2,1,0:T(8,128)(2,1)S(1)}, u32[]{:S(2)}, u32[]{:S(2)}) collective-permute-start(bf16[8,128,128]{2,1,0:T(8,128)(2,1)} %get-tuple-element.161), channel_id=1, source_target_pairs={{0,1},{1,2},{2,3},{3,4},{4,5},{5,6},{6,7},{7,8},{8,9},{9,10},{10,1... | collective-permute-start | bytes 786440 | tf_op jit(solution)/shard_map/ppermute | solution.py:14
  291.1 10.8 %collective-permute-start.1 = (bf16[8,128,128]{2,1,0:T(8,128)(2,1)}, bf16[8,128,128]{2,1,0:T(8,128)(2,1)S(1)}, u32[]{:S(2)}, u32[]{:S(2)}) collective-permute-start(bf16[8,128,128]{2,1,0:T(8,128)(2,1)} %get-tuple-element.160), channel_id=1, source_target_pairs={{1,0},{2,1},{3,2},{4,3},{5,4},{6,5},{7,6},{8,7},{9,8},{10,9},{11,1... | collective-permute-start | bytes 786440 | tf_op jit(solution)/shard_map/ppermute | solution.py:14
  292.6 9.4 collective-permute-start.2
  295.1 7.0 collective-permute-start.3
  305.9 1.9 copy-start.1
  315.1 1.9 copy-start.1
  324.3 1.9 copy-start.1
  333.4 1.9 copy-start.1
  342.6 1.9 copy-start.1
  351.8 1.9 copy-start.1
  360.9 1.9 copy-start.1
  370.1 1.9 copy-start.1
  379.3 1.9 copy-start.1
  386.1 3.6 copy-start.3
  389.6 520.1 %all-reduce.11.cloned.1.call-start = ((), (), s32[]{:S(2)}) async-start(), calls=%async_computation.2 | async-start | bytes 262144 | tf_op jit(solution)/shard_map/psum | solution.py:27
  659.0 105.0 %copy-start.9 = (bf16[4096,128]{1,0:T(8,128)(2,1)}, bf16[4096,128]{1,0:T(8,128)(2,1)S(1)}, u32[]{:S(2)}) copy-start(bf16[4096,128]{1,0:T(8,128)(2,1)S(1)} %convolution_convert_fusion) | copy-start | bytes 3145732
  659.8 6.3 copy-start.8
  659.8 6.3 copy-start.11
  660.0 13.9 %collective-permute-start.5 = (bf16[8,128,128]{2,1,0:T(8,128)(2,1)S(1)}, bf16[8,128,128]{2,1,0:T(8,128)(2,1)S(1)}, u32[]{:S(2)}, u32[]{:S(2)}) collective-permute-start(bf16[8,128,128]{2,1,0:T(8,128)(2,1)S(1)} %get-tuple-element.156), channel_id=1, source_target_pairs={{1,0},{2,1},{3,2},{4,3},{5,4},{6,5},{7,6},{8,7},{9,8},{10,9},{11,1... | collective-permute-start | bytes 786440 | tf_op jit(solution)/shard_map/ppermute | solution.py:14
  661.5 12.4 %collective-permute-start.4 = (bf16[8,128,128]{2,1,0:T(8,128)(2,1)S(1)}, bf16[8,128,128]{2,1,0:T(8,128)(2,1)S(1)}, u32[]{:S(2)}, u32[]{:S(2)}) collective-permute-start(bf16[8,128,128]{2,1,0:T(8,128)(2,1)S(1)} %get-tuple-element.157), channel_id=1, source_target_pairs={{0,1},{1,2},{2,3},{3,4},{4,5},{5,6},{6,7},{7,8},{8,9},{9,10},{10,1... | collective-permute-start | bytes 786440 | tf_op jit(solution)/shard_map/ppermute | solution.py:14
  667.9 7.7 collective-permute-start.6
  670.0 7.5 collective-permute-start.7
  681.2 1.9 copy-start.4
  699.5 1.9 copy-start.4
  766.0 207.3 %all-reduce.13.cloned.1.call-start = ((), (), s32[]{:S(2)}) async-start(), calls=%async_computation.3 | async-start | bytes 262144 | tf_op jit(solution)/shard_map/psum | solution.py:27
  (28 other events, 41.5 us)
Sparse Core Ops, SparseCore 0:
  14.1 243.4 all-reduce.6
  389.7 241.7 all-reduce.8
  766.1 143.4 all-reduce.10
  911.9 61.3 all-reduce.12
